TPU v7x, 32 devices: a whole 2x2x4 slice. The times are simulated.
32 devices in a mesh: grp: 2 (over y), row: 4 (over z), col: 2 (over x), sub: 2 (over core).
Axes of the slice: x: 2, y: 2, z: 4, core: 2. Of those that a mesh axis runs over, the one named last changes fastest.
Arguments:
- homolog_activations: bfloat16 [128, 192, 256], P(('grp', 'col', 'sub'), 'row'), parts along dimension 0, may hold values from -6 to 6
- edge_activations: bfloat16 [384, 192, 128], P(('grp', 'row', 'sub'), 'col'), parts along dimension 0, may hold values from -6 to 6
- first_projection_matrix: bfloat16 [256, 32], replicated, may hold values from -0.375 to 0.375
- second_projection_matrix: bfloat16 [256, 32], replicated, may hold values from -0.375 to 0.375
- tensor_product_matrix: bfloat16 [1024, 128], replicated, may hold values from -1.5 to 1.5
- multiplicative_entry_matrix: bfloat16 [128, 640], replicated, may hold values from -0.5 to 0.5
- multiplicative_exit_matrix: bfloat16 [128, 128], replicated, may hold values from -0.5 to 0.5
Outputs:
- pair_out: bfloat16 [384, 192, 128], P(('grp', 'row', 'sub'), 'col'), parts along dimension 0
There are 2 independent parts, one for each index of `grp`. A program takes and returns all parts, laid end to end along the dimension named above; an argument that names none is the same for every part. Nothing has to cross between parts.
All inputs are finite; a program needn't handle non-finite values.
Results may differ from a plain program's by a relative error of at most 0.012.
Values may be sent and summed in bfloat16 or wider, within the bound.
No kernel may reach another device: no remote copies, remote signals or barrier semaphores. Data moves between devices by JAX's collectives and lax.ppermute only.
A program may use at most 128 MiB of HBM per device.

v0:
```python
import jax
import jax.numpy as jnp
from jax import lax
from jax.sharding import PartitionSpec as P

EPSILON = 1e-05


def standardize_features(values):
    centred = values - jnp.mean(values, axis=-1, keepdims=True)
    spread = jnp.mean(centred * centred, axis=-1, keepdims=True)
    return centred * lax.rsqrt(spread + EPSILON)


def per_device(
    homolog_activations,
    edge_activations,
    first_projection_matrix,
    second_projection_matrix,
    tensor_product_matrix,
    multiplicative_entry_matrix,
    multiplicative_exit_matrix,
):
    homologs_each_device, aminos_each_device, homolog_column_extent = homolog_activations.shape
    tile_rows, tile_cols, width = edge_activations.shape
    factor_width = first_projection_matrix.shape[1]
    sub_count = lax.axis_size("sub")
    col_count = lax.axis_size("col")
    sub_index = lax.axis_index("sub")
    normalized_alignment = (
        standardize_features(homolog_activations.astype(jnp.float32))
        .astype(jnp.bfloat16)
        .reshape(homologs_each_device * aminos_each_device, homolog_column_extent)
    )
    left_factor_slice = jnp.dot(
        normalized_alignment, first_projection_matrix, preferred_element_type=jnp.float32
    ).astype(jnp.bfloat16)
    left_factor_slice = left_factor_slice.reshape(
        homologs_each_device, aminos_each_device * factor_width
    )
    right_factor_slice = jnp.dot(
        normalized_alignment, second_projection_matrix, preferred_element_type=jnp.float32
    ).astype(jnp.bfloat16)
    right_factor_slice = right_factor_slice.reshape(
        homologs_each_device, aminos_each_device * factor_width
    )
    right_residues = lax.all_gather(right_factor_slice, "row", axis=1, tiled=True)
    column_groups = right_residues.reshape(
        homologs_each_device, col_count, tile_cols * factor_width
    ).transpose(1, 0, 2)
    right_outgoing = jnp.broadcast_to(
        column_groups[:, None],
        (col_count, sub_count, homologs_each_device, tile_cols * factor_width),
    )
    right_outgoing = right_outgoing.reshape(
        col_count * sub_count, homologs_each_device, tile_cols * factor_width
    )
    right_all = lax.all_to_all(
        right_outgoing, ("col", "sub"), split_axis=0, concat_axis=1, tiled=True
    )[0]
    left_all = lax.all_gather(left_factor_slice, ("col", "sub"), axis=0, tiled=True)
    left_rows = lax.dynamic_slice_in_dim(
        left_all, sub_index * (tile_rows * factor_width), tile_rows * factor_width, 1
    )
    seq_total = left_rows.shape[0]
    outer = (
        lax.dot_general(
            left_rows, right_all, (((0,), (0,)), ((), ())), preferred_element_type=jnp.float32
        )
        / seq_total
    )
    outer = outer.astype(jnp.bfloat16).reshape(tile_rows, factor_width, tile_cols, factor_width)
    outer = outer.transpose(0, 2, 1, 3).reshape(tile_rows * tile_cols, factor_width * factor_width)
    pair_flat = edge_activations.reshape(tile_rows * tile_cols, width).astype(jnp.float32)
    pair_mid = (
        pair_flat + jnp.dot(outer, tensor_product_matrix, preferred_element_type=jnp.float32)
    ).astype(jnp.bfloat16)
    pair_normed = standardize_features(pair_mid.astype(jnp.float32)).astype(jnp.bfloat16)
    projected = jnp.dot(
        pair_normed, multiplicative_entry_matrix, preferred_element_type=jnp.float32
    )
    left_tri = (jax.nn.sigmoid(projected[:, width : 2 * width]) * projected[:, :width]).astype(
        jnp.bfloat16
    )
    right_tri = (
        jax.nn.sigmoid(projected[:, 3 * width : 4 * width]) * projected[:, 2 * width : 3 * width]
    ).astype(jnp.bfloat16)
    out_gate = jax.nn.sigmoid(projected[:, 4 * width :])
    left_tile = left_tri.reshape(tile_rows, tile_cols, width).transpose(2, 0, 1)
    right_tile = right_tri.reshape(tile_rows, tile_cols, width).transpose(2, 0, 1)
    left_chan, right_chan = (
        lax.all_to_all(left_tile, ("row", "sub"), split_axis=0, concat_axis=1, tiled=True),
        lax.all_to_all(right_tile, ("row", "sub"), split_axis=0, concat_axis=1, tiled=True),
    )
    right_block = lax.all_to_all(right_chan, "col", split_axis=1, concat_axis=2, tiled=True)
    channels = jnp.einsum(
        "gik,gjk->gij",
        lax.all_gather(left_chan, "col", axis=2, tiled=True),
        right_block,
        preferred_element_type=jnp.float32,
    ).astype(jnp.bfloat16)
    tiles = lax.all_to_all(channels, ("row", "sub"), split_axis=1, concat_axis=0, tiled=True)
    tri = tiles.transpose(1, 2, 0).reshape(tile_rows * tile_cols, width)
    tri_normed = standardize_features(tri.astype(jnp.float32)).astype(jnp.bfloat16)
    update = jnp.dot(tri_normed, multiplicative_exit_matrix, preferred_element_type=jnp.float32)
    result = (pair_mid.astype(jnp.float32) + out_gate * update).astype(jnp.bfloat16)
    return result.reshape(tile_rows, tile_cols, width)


def solution(mesh):
    in_specs = (
        P(("grp", "col", "sub"), "row", None),
        P(("grp", "row", "sub"), "col", None),
        P(),
        P(),
        P(),
        P(),
        P(),
    )
    out_specs = P(("grp", "row", "sub"), "col", None)
    return jax.shard_map(
        per_device, mesh=mesh, in_specs=in_specs, out_specs=out_specs, check_vma=False
    )
```

profile of v0, /device:TPU:0, one launch (start us, length us, event | category | flops | bytes accessed | tf_op | source)
XLA Modules:
  0.0 214.5 jit_solution(9777505988347257659)
XLA Ops:
  6.5 1.2 convert_reduce_fusion
  7.8 1.3 fusion.24
  9.1 1.3 fusion.25
  11.0 15.5 %all_gather.10 = bf16[16,6144]{1,0:T(8,128)(2,1)S(1)} all-gather(bf16[16,1536]{1,0:T(8,128)(2,1)S(1)} %reshape.103), channel_id=1, replica_groups=mesh['grp'=2,'row'=4,'col'=2,'sub'=2] {'row'}, dimensions={1}, use_global_device_ids=true | all-gather | bytes 245760 | tf_op jit(solution)/shard_map/all_gather | solution.py:47
  26.7 0.8 broadcast_in_dim.2
  27.5 3.5 %all-to-all-start = ((bf16[4,16,3072]{2,1,0:T(8,128)(2,1)}), bf16[4,16,3072]{2,1,0:T(8,128)(2,1)S(1)}, u32[]{:S(2)}, u32[]{:S(2)}) async-start(bf16[4,16,3072]{2,1,0:T(8,128)(2,1)} %bitcast.3), calls=%async_computation | async-start | bytes 786432 | tf_op jit(solution)/shard_map/all_to_all | solution.py:58
  31.6 8.6 %all_gather.9 = bf16[64,1536]{1,0:T(8,128)(2,1)S(1)} all-gather(bf16[16,1536]{1,0:T(8,128)(2,1)S(1)} %reshape.102), channel_id=1, replica_groups=mesh['grp'=2,'row'=4,'col'=2,'sub'=2] {'col','sub'}, dimensions={0}, use_global_device_ids=true | all-gather | bytes 245760 | tf_op jit(solution)/shard_map/all_gather | solution.py:61
  40.2 3.6 %multiply_convert_fusion = bf16[768,3072]{1,0:T(8,128)(2,1)} fusion(bf16[64,3072]{1,0:T(8,128)(2,1)S(1)} %bitcast.66, bf16[64,1536]{1,0:T(8,128)(2,1)S(1)} %all_gather.9, s32[]{:T(128)S(6)} %select_n.3), kind=kOutput, calls=%fused_computation | convolution fusion | flops 306708480 | bytes 5210116 | tf_op jit(solution)/shard_map/dot_general | solution.py:67
  43.8 21.3 %reshape.106 = bf16[24,32,96,32]{3,2,1,0:T(8,128)(2,1)} reshape(bf16[768,3072]{1,0:T(8,128)(2,1)} %multiply_convert_fusion) | data formatting | bytes 9437184 | tf_op jit(solution)/shard_map/reshape | solution.py:72
  65.1 16.4 %copy.38 = bf16[24,96,32,32]{1,0,3,2:T(8,128)(2,1)} copy(bf16[24,96,32,32]{3,1,2,0:T(8,128)(2,1)} %bitcast.53) | data formatting | bytes 9437184 | tf_op jit(solution)/shard_map/transpose | solution.py:73
  81.5 10.3 %reshape.107 = bf16[2304,1024]{0,1:T(8,128)(2,1)} reshape(bf16[24,96,32,32]{1,0,3,2:T(8,128)(2,1)} %copy.38) | data formatting | bytes 9437184 | tf_op jit(solution)/shard_map/reshape | solution.py:73
  91.8 4.0 %fusion.31 = (f32[2304]{0:T(1024)S(1)}, f32[2304,128]{1,0:T(8,128)S(1)}) fusion(bf16[2304,1024]{0,1:T(8,128)(2,1)} %reshape.107, bf16[1024,128]{1,0:T(8,128)(2,1)S(1)} %copy-done, bf16[2304,128]{1,0:T(8,128)(2,1)S(1)} %bitcast.68), kind=kOutput, calls=%fused_computation.52 | convolution fusion | flops 605452032 | bytes 6759424 | tf_op jit(solution)/shard_map/dot_general | solution.py:76
  95.8 0.7 multiply_reduce_fusion.1
  96.7 1.1 fusion.26
  97.8 0.6 fusion.13
  98.4 1.9 copy-done.1
  100.3 1.3 copy.39
  101.5 4.9 %all-to-all-start.1 = ((bf16[128,24,96]{2,1,0:T(8,128)(2,1)}), bf16[128,24,96]{2,1,0:T(8,128)(2,1)S(1)}, u32[]{:S(2)}, u32[]{:S(2)}) async-start(bf16[128,24,96]{2,1,0:T(8,128)(2,1)} %bitcast.7), calls=%async_computation.1 | async-start | bytes 1572864 | tf_op jit(solution)/shard_map/all_to_all | solution.py:92
  106.5 1.3 copy.42
  107.7 19.7 %all-to-all-done.1 = bf16[128,24,96]{2,1,0:T(8,128)(2,1)S(1)} async-done(((bf16[128,24,96]{2,1,0:T(8,128)(2,1)}), bf16[128,24,96]{2,1,0:T(8,128)(2,1)S(1)}, u32[]{:S(2)}, u32[]{:S(2)}) %all-to-all-start.1) | async-done | bytes 589856 | tf_op jit(solution)/shard_map/all_to_all | solution.py:92
  127.4 3.5 %all-to-all-start.2 = ((bf16[128,24,96]{2,1,0:T(8,128)(2,1)}), bf16[128,24,96]{2,1,0:T(8,128)(2,1)S(1)}, u32[]{:S(2)}, u32[]{:S(2)}) async-start(bf16[128,24,96]{2,1,0:T(8,128)(2,1)} %bitcast.62), calls=%async_computation.2 | async-start | bytes 1572864 | tf_op jit(solution)/shard_map/all_to_all | solution.py:93
  131.2 1.0 copy.40
  132.2 3.1 %copy.41 = bf16[16,192,96]{1,0,2:T(8,128)(2,1)} copy(bf16[16,192,96]{2,1,0:T(8,128)(2,1)} %bitcast.59) | data formatting | bytes 1179648 | tf_op jit(solution)/shard_map/all_to_all | solution.py:92
  135.3 16.5 %all-to-all-done.2 = bf16[128,24,96]{2,1,0:T(8,128)(2,1)S(1)} async-done(((bf16[128,24,96]{2,1,0:T(8,128)(2,1)}), bf16[128,24,96]{2,1,0:T(8,128)(2,1)S(1)}, u32[]{:S(2)}, u32[]{:S(2)}) %all-to-all-start.2) | async-done | bytes 589856 | tf_op jit(solution)/shard_map/all_to_all | solution.py:93
  152.0 0.5 copy.44
  152.5 18.6 %all_to_all.75 = bf16[16,192,96]{2,0,1:T(8,128)(2,1)S(1)} all-to-all(bf16[16,192,96]{2,0,1:T(8,128)(2,1)S(1)} %copy.44), channel_id=1, replica_groups=mesh['grp'=2,'row'=4,'col'=2,'sub'=2] {'col'}, dimensions={1} | all-to-all | bytes 1179648 | tf_op jit(solution)/shard_map/all_to_all | solution.py:95
  171.1 0.8 copy.46
  172.4 2.2 %fusion.6 = bf16[16,192,96]{2,1,0:T(8,128)(2,1)S(1)} fusion(bf16[16,96,192]{2,1,0:T(8,128)(2,1)S(1)} %all_to_all.67, bf16[16,192,192]{1,0,2:T(8,128)(2,1)} %all-gather.2.cloned.1.call-done), kind=kOutput, calls=%fused_computation.10 | convolution fusion | flops 113541120 | bytes 2359296 | tf_op jit(solution)/shard_map/gik,gjk->gij/dot_general | solution.py:96
  175.2 25.3 %all_to_all.76 = bf16[16,192,96]{2,0,1:T(8,128)(2,1)S(1)} all-to-all(bf16[16,192,96]{2,0,1:T(8,128)(2,1)S(1)} %copy.48), channel_id=1, replica_groups=mesh['grp'=2,'row'=4,'col'=2,'sub'=2] {'row','sub'}, dimensions={1} | all-to-all | bytes 1179648 | tf_op jit(solution)/shard_map/all_to_all | solution.py:102
  201.2 1.5 copy.50
  202.8 2.4 %fusion.21 = bf16[2304,128]{1,0:T(8,128)(2,1)S(1)} fusion(f32[24,96,128]{2,1,0:T(8,128)} %copy.50, f32[2304]{0:T(1024)S(1)} %rsqrt.30, f32[2304]{0:T(1024)S(1)} %div.45), kind=kLoop, calls=%fused_computation.29 | loop fusion | flops 884736 | bytes 1787904 | tf_op jit(solution)/shard_map/convert_element_type | solution.py:104
  205.2 2.5 %fusion.1 = bf16[2304,128]{1,0:T(8,128)(2,1)} fusion(f32[2304,128]{1,0:T(8,128)S(1)} %get-tuple-element.8, bf16[2304,128]{1,0:T(8,128)(2,1)S(1)} %fusion.21, bf16[128,128]{1,0:T(8,128)(2,1)S(1)} %copy-done.6, f32[2304,640]{1,0:T(8,128)} %copy-done.1), kind=kOutput, calls=%fused_computation.4 | convolution fusion | flops 77266944 | bytes 3571712 | tf_op jit(solution)/shard_map/dot_general | solution.py:105
  (39 shorter events, 3.7 us)
Async XLA Ops:
  6.5 85.2 %copy-start = (bf16[1024,128]{1,0:T(8,128)(2,1)S(1)}, bf16[1024,128]{1,0:T(8,128)(2,1)}, u32[]{:S(2)}) copy-start(bf16[1024,128]{1,0:T(8,128)(2,1)} %param.11) | copy-start | bytes 786436
  6.5 3.9 %copy-start.4 = (bf16[256,32]{0,1:T(8,128)(2,1)S(1)}, bf16[256,32]{0,1:T(8,128)(2,1)}, u32[]{:S(2)}) copy-start(bf16[256,32]{0,1:T(8,128)(2,1)} %param.10) | copy-start | bytes 49156
  11.0 19.9 %copy-start.5 = (bf16[256,32]{0,1:T(8,128)(2,1)S(1)}, bf16[256,32]{0,1:T(8,128)(2,1)}, u32[]{:S(2)}) copy-start(bf16[256,32]{0,1:T(8,128)(2,1)} %param.9) | copy-start | bytes 49156
  27.5 12.7 %all-to-all-start = ((bf16[4,16,3072]{2,1,0:T(8,128)(2,1)}), bf16[4,16,3072]{2,1,0:T(8,128)(2,1)S(1)}, u32[]{:S(2)}, u32[]{:S(2)}) async-start(bf16[4,16,3072]{2,1,0:T(8,128)(2,1)} %bitcast.3), calls=%async_computation | async-start | bytes 786432 | tf_op jit(solution)/shard_map/all_to_all | solution.py:58
  81.4 10.3 %copy-start.2 = (bf16[24,96,128]{2,1,0:T(8,128)(2,1)S(1)}, bf16[24,96,128]{2,1,0:T(8,128)(2,1)}, u32[]{:S(2)}) copy-start(bf16[24,96,128]{2,1,0:T(8,128)(2,1)} %param.8) | copy-start | bytes 1769476
  95.7 0.9 copy-start.3
  97.8 2.5 %copy-start.1 = (f32[2304,640]{1,0:T(8,128)}, f32[2304,640]{1,0:T(8,128)S(1)}, u32[]{:S(2)}) copy-start(f32[2304,640]{1,0:T(8,128)S(1)} %fusion.26) | copy-start | bytes 17694724
  101.5 25.9 %all-to-all-start.1 = ((bf16[128,24,96]{2,1,0:T(8,128)(2,1)}), bf16[128,24,96]{2,1,0:T(8,128)(2,1)S(1)}, u32[]{:S(2)}, u32[]{:S(2)}) async-start(bf16[128,24,96]{2,1,0:T(8,128)(2,1)} %bitcast.7), calls=%async_computation.1 | async-start | bytes 1572864 | tf_op jit(solution)/shard_map/all_to_all | solution.py:92
  127.4 24.4 %all-to-all-start.2 = ((bf16[128,24,96]{2,1,0:T(8,128)(2,1)}), bf16[128,24,96]{2,1,0:T(8,128)(2,1)S(1)}, u32[]{:S(2)}, u32[]{:S(2)}) async-start(bf16[128,24,96]{2,1,0:T(8,128)(2,1)} %bitcast.62), calls=%async_computation.2 | async-start | bytes 1572864 | tf_op jit(solution)/shard_map/all_to_all | solution.py:93
  131.0 41.4 %all-gather.2.cloned.1.call-start = ((), (), s32[]{:S(2)}) async-start(), calls=%async_computation.5 | async-start | bytes 2359296 | tf_op jit(solution)/shard_map/all_gather | solution.py:98
  202.8 2.4 %copy-start.6 = (bf16[128,128]{1,0:T(8,128)(2,1)S(1)}, bf16[128,128]{1,0:T(8,128)(2,1)}, u32[]{:S(2)}) copy-start(bf16[128,128]{1,0:T(8,128)(2,1)} %param.13) | copy-start | bytes 98308
Sparse Core Ops, SparseCore 0:
  135.5 32.6 all-gather.1
where the time goes:
time: 216 us; the launch traced here: 215 us
  blocking collectives  68.1 us (32%)
  local copies, waits for them, and re-layouts  62.6 us (29%)
  waiting for transfers between devices  36.2 us (17%)
  matrix products  13.9 us (6%)
  between operations  13.6 us (6%)
  starting transfers between devices  12.2 us (6%)
  other arithmetic  7.95 us (4%)
    all_to_all x1, blocking collectives, per_device(): lax.all_to_all(channels, ('row', 'sub'), split_axis=1, concat_axis=0, til...  25.3 us
    reshape x1, local copies, waits for them, and re-layouts, per_device(): outer.astype(jnp.bfloat16)  21.3 us
    all_to_all x1, waiting for transfers between devices, per_device(): lax.all_to_all(left_tile, ('row', 'sub'), split_axis=0, concat_axis=1, ti...  19.7 us
    all_to_all x1, blocking collectives, per_device(): lax.all_to_all(right_chan, 'col', split_axis=1, concat_axis=2, tiled=True)  18.6 us
    all_to_all x1, waiting for transfers between devices, per_device(): lax.all_to_all(right_tile, ('row', 'sub'), split_axis=0, concat_axis=1, t...  16.5 us
    transpose x1, local copies, waits for them, and re-layouts, per_device(): outer.transpose(0, 2, 1, 3)  16.4 us
    all_gather x1, blocking collectives, per_device(): lax.all_gather(right_factor_slice, 'row', axis=1, tiled=True)  15.5 us
    reshape x1, local copies, waits for them, and re-layouts, per_device(): outer.transpose(0, 2, 1, 3)  10.3 us
  transfers between devices with their start and end apart: 4, of which 2 were waited for; matrix products, arithmetic and copies ran while one was open for 3% of the time, Pallas kernels for 0%

commit v1 on v0

--- a/solution.py
+++ b/solution.py
@@ -1,15 +1,87 @@
-import jax
-import jax.numpy as jnp
+import functools
+import jax, jax.numpy as jnp
 from jax import lax
+from jax.experimental import pallas as pl
+from jax.experimental.pallas import tpu as pltpu
 from jax.sharding import PartitionSpec as P
-
 EPSILON = 1e-05
+def ln0(x):
+    m=jnp.mean(x,axis=0,keepdims=True); d=x-m
+    v=jnp.mean(d*d,axis=0,keepdims=True)
+    return d*lax.rsqrt(v+EPSILON)
 
 
 def standardize_features(values):
     centred = values - jnp.mean(values, axis=-1, keepdims=True)
     spread = jnp.mean(centred * centred, axis=-1, keepdims=True)
     return centred * lax.rsqrt(spread + EPSILON)
+
+
+def prep_kernel(fw, r_ref, rt_ref, sc):
+    S, JB = r_ref.shape
+    J = JB//fw
+    blk = 128
+    w = sc.shape[2]
+    for u in range(S//w):
+        for t in range(JB//blk):
+            sc[u, t*blk:(t+1)*blk, :] = r_ref[u*w:(u+1)*w, t*blk:(t+1)*blk].astype(jnp.float32).T
+        for b in range(fw):
+            rt_ref[b, :, u*w:(u+1)*w] = sc[u, pl.ds(b, J, stride=fw), :].astype(jnp.bfloat16)
+
+def prep(r, fw):
+    S, JB = r.shape
+    J = JB//fw
+    w = min(S, 128)
+    return pl.pallas_call(functools.partial(prep_kernel, fw),
+      out_shape=jax.ShapeDtypeStruct((fw, J, S), jnp.bfloat16),
+      in_specs=[pl.BlockSpec(memory_space=pltpu.VMEM)],
+      out_specs=pl.BlockSpec(memory_space=pltpu.VMEM),
+      scratch_shapes=[pltpu.VMEM((S//w, JB, w), jnp.float32)],
+    )(r)
+
+def a_kernel(cfg, l_ref, rt_ref, wt_ref, e_ref, went_ref, *rest):
+    fw, C, TI, J, S = cfg
+    mid_ref, gate_ref, lo_ref, ro_ref, lt, ot, lsc, rsc = rest
+    g = pl.program_id(0)
+    IG = l_ref.shape[1]//fw
+    for t in range(IG*fw//128):
+        lt[t*128:(t+1)*128,:] = l_ref[:, t*128:(t+1)*128].astype(jnp.float32).T.astype(jnp.bfloat16)
+    ltv = lt[...]
+    for b in range(fw):
+        o = lax.dot_general(ltv, rt_ref[b], (((1,),(1,)),((),())), preferred_element_type=jnp.float32)
+        ob = o.astype(jnp.bfloat16)
+        for i in range(IG):
+            ot[i, b*fw:(b+1)*fw, :] = ob[i*fw:(i+1)*fw, :]
+    wt = wt_ref[...]; we = went_ref[...]
+    for i in range(IG):
+        pt = lax.dot_general(wt, ot[i], (((1,),(0,)),((),())), preferred_element_type=jnp.float32)
+        et = e_ref[i].astype(jnp.float32).T
+        mid = (et + pt*(1.0/S)).astype(jnp.bfloat16)
+        mid_ref[i] = mid
+        nt = ln0(mid.astype(jnp.float32)).astype(jnp.bfloat16)
+        p = lax.dot_general(we, nt, (((1,),(0,)),((),())), preferred_element_type=jnp.float32)
+        lsc[i] = jax.nn.sigmoid(p[C:2*C])*p[:C]
+        rsc[i] = jax.nn.sigmoid(p[3*C:4*C])*p[2*C:3*C]
+        gate_ref[i] = jax.nn.sigmoid(p[4*C:])
+    lo_ref[...] = pltpu.einshape("icj->cij", lsc[...]).astype(jnp.bfloat16)
+    ro_ref[...] = pltpu.einshape("icj->cij", rsc[...]).astype(jnp.bfloat16)
+
+def a_call(l, rt, wt, e, went, IG=8):
+    S,IA=l.shape; fw,J,_=rt.shape; TI=IA//fw; C=wt.shape[0]
+    cfg=(fw,C,TI,J,S)
+    f=pl.pallas_call(functools.partial(a_kernel,cfg), grid=(TI//IG,),
+      out_shape=(jax.ShapeDtypeStruct((TI,C,J),jnp.bfloat16),jax.ShapeDtypeStruct((TI,C,J),jnp.float32),
+                 jax.ShapeDtypeStruct((C,TI,J),jnp.bfloat16),jax.ShapeDtypeStruct((C,TI,J),jnp.bfloat16)),
+      in_specs=[pl.BlockSpec((S,IG*fw),lambda g:(0,g)),
+        pl.BlockSpec((fw,J,S),lambda g:(0,0,0)),pl.BlockSpec(wt.shape,lambda g:(0,0)),
+        pl.BlockSpec((IG,J,C),lambda g:(g,0,0)),pl.BlockSpec(went.shape,lambda g:(0,0))],
+      out_specs=(pl.BlockSpec((IG,C,J),lambda g:(g,0,0)),pl.BlockSpec((IG,C,J),lambda g:(g,0,0)),
+        pl.BlockSpec((C,IG,J),lambda g:(0,g,0)),pl.BlockSpec((C,IG,J),lambda g:(0,g,0))),
+      scratch_shapes=[pltpu.VMEM((IG*fw,S),jnp.bfloat16),pltpu.VMEM((IG,fw*fw,J),jnp.bfloat16),
+        pltpu.VMEM((IG,C,J),jnp.float32),pltpu.VMEM((IG,C,J),jnp.float32)],
+      compiler_params=pltpu.CompilerParams(vmem_limit_bytes=60*1024*1024),
+    )
+    return f(l,rt,wt,e,went)
 
 
 def per_device(
@@ -62,32 +134,17 @@
     left_rows = lax.dynamic_slice_in_dim(
         left_all, sub_index * (tile_rows * factor_width), tile_rows * factor_width, 1
     )
-    seq_total = left_rows.shape[0]
-    outer = (
-        lax.dot_general(
-            left_rows, right_all, (((0,), (0,)), ((), ())), preferred_element_type=jnp.float32
-        )
-        / seq_total
+    right_prepared = prep(right_all, factor_width)
+    outer_weight = (
+        tensor_product_matrix.reshape(factor_width, factor_width, width)
+        .transpose(2, 1, 0)
+        .reshape(width, factor_width * factor_width)
     )
-    outer = outer.astype(jnp.bfloat16).reshape(tile_rows, factor_width, tile_cols, factor_width)
-    outer = outer.transpose(0, 2, 1, 3).reshape(tile_rows * tile_cols, factor_width * factor_width)
-    pair_flat = edge_activations.reshape(tile_rows * tile_cols, width).astype(jnp.float32)
-    pair_mid = (
-        pair_flat + jnp.dot(outer, tensor_product_matrix, preferred_element_type=jnp.float32)
-    ).astype(jnp.bfloat16)
-    pair_normed = standardize_features(pair_mid.astype(jnp.float32)).astype(jnp.bfloat16)
-    projected = jnp.dot(
-        pair_normed, multiplicative_entry_matrix, preferred_element_type=jnp.float32
+    mid_t, gate_t, left_tile, right_tile = a_call(
+        left_rows, right_prepared, outer_weight, edge_activations, multiplicative_entry_matrix.T
     )
-    left_tri = (jax.nn.sigmoid(projected[:, width : 2 * width]) * projected[:, :width]).astype(
-        jnp.bfloat16
-    )
-    right_tri = (
-        jax.nn.sigmoid(projected[:, 3 * width : 4 * width]) * projected[:, 2 * width : 3 * width]
-    ).astype(jnp.bfloat16)
-    out_gate = jax.nn.sigmoid(projected[:, 4 * width :])
-    left_tile = left_tri.reshape(tile_rows, tile_cols, width).transpose(2, 0, 1)
-    right_tile = right_tri.reshape(tile_rows, tile_cols, width).transpose(2, 0, 1)
+    pair_mid = mid_t.transpose(0, 2, 1).reshape(tile_rows * tile_cols, width)
+    out_gate = gate_t.transpose(0, 2, 1).reshape(tile_rows * tile_cols, width)
     left_chan, right_chan = (
         lax.all_to_all(left_tile, ("row", "sub"), split_axis=0, concat_axis=1, tiled=True),
         lax.all_to_all(right_tile, ("row", "sub"), split_axis=0, concat_axis=1, tiled=True),

time: 216 us -> 170 us (0.79)
  local copies, waits for them, and re-layouts: 62.6 us -> 16.7 us
  Pallas kernels: 0 us -> 15.9 us
  matrix products: 13.9 us -> 3.83 us
  blocking collectives: 68.1 us -> 65 us
    reshape x4 -> x1, local copies, waits for them, and re-layouts: 34.1 us -> 0.88 us  [per_device(): outer_weight = tensor_product_matrix.reshape(factor_width, factor_width,...]
    pallas_call x0 -> x2, Pallas kernels: none -> 15.9 us  [the longest x1 12.8 us: a_call(): return f(l, rt, wt, e, went)]
    transpose x1 -> x2, local copies, waits for them, and re-layouts: 16.4 us -> 2.99 us  [the longest x1 2.89 us: per_device(): out_gate = gate_t.transpose(0, 2, 1).reshape(tile_rows * tile_cols, width)]
    dot_general x3 -> x0, matrix products: 8.65 us -> none  [the longest x1 3.97 us: per_device(): jnp.dot(outer, tensor_product_matrix, preferred_element_type=jnp.float32)]
    all_to_all x1, waiting for transfers between devices: 19.7 us -> 17.5 us  [per_device(): lax.all_to_all(channels, ('row', 'sub'), split_axis=1, concat_axis=0, til...]
  transfers between devices with their start and end apart: 4 -> 4, of which waited for: 2 -> 2; matrix products, arithmetic and copies ran while one was open for 3% -> 6% of each run, Pallas kernels for 0% -> 0%
where the time goes in v1:
time: 170 us
  blocking collectives  65 us (38%)
  waiting for transfers between devices  36.2 us (21%)
  local copies, waits for them, and re-layouts  16.7 us (10%)
  Pallas kernels  15.9 us (9%)
  between operations  13.6 us (8%)
  starting transfers between devices  11.7 us (7%)
  other arithmetic  6.84 us (4%)
  matrix products  3.83 us (2%)
    all_to_all x1, blocking collectives, per_device(): lax.all_to_all(left_tile, ('row', 'sub'), split_axis=0, concat_axis=1, ti...  25.9 us
    all_to_all x1, waiting for transfers between devices, per_device(): lax.all_to_all(right_tile, ('row', 'sub'), split_axis=0, concat_axis=1, t...  18.6 us
    all_to_all x1, waiting for transfers between devices, per_device(): lax.all_to_all(channels, ('row', 'sub'), split_axis=1, concat_axis=0, til...  17.5 us
    all_to_all x1, blocking collectives, per_device(): lax.all_to_all(right_chan, 'col', split_axis=1, concat_axis=2, tiled=True)  16.9 us
    all_gather x1, blocking collectives, per_device(): lax.all_gather(right_factor_slice, 'row', axis=1, tiled=True)  15.5 us
    pallas_call x1, Pallas kernels, a_call(): return f(l, rt, wt, e, went)  12.8 us
    all_gather x1, blocking collectives, per_device(): lax.all_gather(left_factor_slice, ('col', 'sub'), axis=0, tiled=True)  6.8 us
    all_to_all x1, starting transfers between devices, per_device(): lax.all_to_all(channels, ('row', 'sub'), split_axis=1, concat_axis=0, til...  4.61 us
  transfers between devices with their start and end apart: 4, of which 2 were waited for; matrix products, arithmetic and copies ran while one was open for 6% of the time, Pallas kernels for 0%

profile of v1, /device:TPU:0, one launch (start us, length us, event | category | flops | bytes accessed | tf_op | source)
XLA Modules:
  0.0 169.8 jit_solution(2629590321475699297)
XLA Ops:
  6.5 1.2 convert_reduce_fusion
  7.7 1.3 fusion.11
  9.1 1.3 fusion.12
  11.0 15.5 %all_gather.10 = bf16[16,6144]{1,0:T(8,128)(2,1)S(1)} all-gather(bf16[16,1536]{1,0:T(8,128)(2,1)S(1)} %reshape.88), channel_id=1, replica_groups=mesh['grp'=2,'row'=4,'col'=2,'sub'=2] {'row'}, dimensions={1}, use_global_device_ids=true | all-gather | bytes 245760 | tf_op jit(solution)/shard_map/all_gather | solution.py:119
  26.7 0.8 broadcast_in_dim.2
  27.4 3.5 %all-to-all-start = ((bf16[4,16,3072]{2,1,0:T(8,128)(2,1)}), bf16[4,16,3072]{2,1,0:T(8,128)(2,1)S(1)}, u32[]{:S(2)}, u32[]{:S(2)}) async-start(bf16[4,16,3072]{2,1,0:T(8,128)(2,1)} %bitcast.2), calls=%async_computation | async-start | bytes 786432 | tf_op jit(solution)/shard_map/all_to_all | solution.py:130
  31.7 0.9 copy.59.wt_ref
  32.5 0.8 copy.58
  33.4 6.8 %all_gather.9 = bf16[64,1536]{1,0:T(8,128)(2,1)S(1)} all-gather(bf16[16,1536]{1,0:T(8,128)(2,1)S(1)} %reshape.87), channel_id=1, replica_groups=mesh['grp'=2,'row'=4,'col'=2,'sub'=2] {'col','sub'}, dimensions={0}, use_global_device_ids=true | all-gather | bytes 245760 | tf_op jit(solution)/shard_map/all_gather | solution.py:133
  40.2 0.6 constant_dynamic-slice_fusion.l_ref
  40.8 0.7 copy-done.2
  41.6 3.1 %shard_map.73.rt_ref = bf16[32,96,64]{2,1,0:T(8,128)(2,1)} custom-call(bf16[64,3072]{1,0:T(8,128)(2,1)} %bitcast.58), custom_call_target="tpu_custom_call" | custom-call | tf_op jit(solution)/shard_map/pallas_call | solution.py:35
  44.7 12.8 %shard_map.74 = (bf16[24,128,96]{2,1,0:T(8,128)(2,1)}, f32[24,128,96]{2,1,0:T(8,128)}, bf16[128,24,96]{2,1,0:T(8,128)(2,1)}, bf16[128,24,96]{2,1,0:T(8,128)(2,1)}) custom-call(bf16[64,768]{1,0:T(8,128)(2,1)} %constant_dynamic-slice_fusion.l_ref, bf16[32,96,64]{2,1,0:T(8,128)(2,1)} %shard_map.73.rt_ref, bf16[128,1024]{1,0:T(8,128)(2,1)} %copy.59.wt_ref, ...), custom_call_target="tpu_custom_call" | custom-call | tf_op jit(solution)/shard_map/pallas_call | solution.py:84
  57.4 25.9 %all_to_all.75 = bf16[128,24,96]{2,1,0:T(8,128)(2,1)S(1)} all-to-all(bf16[128,24,96]{2,1,0:T(8,128)(2,1)} %get-tuple-element.11), channel_id=1, replica_groups=mesh['grp'=2,'row'=4,'col'=2,'sub'=2] {'row','sub'}, dimensions={0} | all-to-all | bytes 1179648 | tf_op jit(solution)/shard_map/all_to_all | solution.py:149
  83.3 3.5 %all-to-all-start.2 = ((bf16[128,24,96]{2,1,0:T(8,128)(2,1)}), bf16[128,24,96]{2,1,0:T(8,128)(2,1)S(1)}, u32[]{:S(2)}, u32[]{:S(2)}) async-start(bf16[128,24,96]{2,1,0:T(8,128)(2,1)} %get-tuple-element.12), calls=%async_computation.2 | async-start | bytes 1572864 | tf_op jit(solution)/shard_map/all_to_all | solution.py:150
  87.0 2.1 %copy.63 = bf16[16,192,96]{1,0,2:T(8,128)(2,1)} copy(bf16[16,192,96]{2,1,0:T(8,128)(2,1)S(1)} %bitcast.55) | data formatting | bytes 1179648 | tf_op jit(solution)/shard_map/all_to_all | solution.py:149
  89.1 18.6 %all-to-all-done.2 = bf16[128,24,96]{2,1,0:T(8,128)(2,1)S(1)} async-done(((bf16[128,24,96]{2,1,0:T(8,128)(2,1)}), bf16[128,24,96]{2,1,0:T(8,128)(2,1)S(1)}, u32[]{:S(2)}, u32[]{:S(2)}) %all-to-all-start.2) | async-done | bytes 589856 | tf_op jit(solution)/shard_map/all_to_all | solution.py:150
  107.8 0.5 copy.65
  108.4 16.9 %all_to_all.76 = bf16[16,192,96]{2,0,1:T(8,128)(2,1)S(1)} all-to-all(bf16[16,192,96]{2,0,1:T(8,128)(2,1)S(1)} %copy.65), channel_id=1, replica_groups=mesh['grp'=2,'row'=4,'col'=2,'sub'=2] {'col'}, dimensions={1} | all-to-all | bytes 1179648 | tf_op jit(solution)/shard_map/all_to_all | solution.py:152
  125.3 0.8 copy.67
  126.1 0.4 all_to_all.67
  126.6 2.2 %fusion.4 = bf16[16,192,96]{2,1,0:T(8,128)(2,1)S(1)} fusion(bf16[16,96,192]{2,1,0:T(8,128)(2,1)S(1)} %all_to_all.67, bf16[16,192,192]{1,0,2:T(8,128)(2,1)} %all-gather.2.cloned.1.call-done), kind=kOutput, calls=%fused_computation.7 | convolution fusion | flops 113541120 | bytes 2359296 | tf_op jit(solution)/shard_map/gik,gjk->gij/dot_general | solution.py:153
  128.8 1.4 copy.69
  130.2 4.6 %all-to-all-start.4 = ((bf16[16,192,96]{2,0,1:T(8,128)(2,1)}), bf16[16,192,96]{2,0,1:T(8,128)(2,1)}, u32[]{:S(2)}, u32[]{:S(2)}) async-start(bf16[16,192,96]{2,0,1:T(8,128)(2,1)} %copy.69), calls=%async_computation.4 | async-start | bytes 1572864 | tf_op jit(solution)/shard_map/all_to_all | solution.py:159
  135.0 0.5 copy.60
  135.5 2.9 %copy.61 = f32[24,96,128]{2,1,0:T(8,128)} copy(f32[24,96,128]{1,2,0:T(8,128)} %bitcast.59) | data formatting | bytes 2359296 | tf_op jit(solution)/shard_map/transpose | solution.py:147
  138.4 17.5 %all-to-all-done.4 = bf16[16,192,96]{2,0,1:T(8,128)(2,1)} async-done(((bf16[16,192,96]{2,0,1:T(8,128)(2,1)}), bf16[16,192,96]{2,0,1:T(8,128)(2,1)}, u32[]{:S(2)}, u32[]{:S(2)}) %all-to-all-start.4) | async-done | bytes 589856 | tf_op jit(solution)/shard_map/all_to_all | solution.py:159
  155.9 1.3 copy.70
  157.3 0.3 multiply_reduce_fusion
  157.8 1.5 copy.71
  159.3 2.5 %fusion.8 = bf16[2304,128]{1,0:T(8,128)(2,1)S(1)} fusion(f32[24,96,128]{2,1,0:T(8,128)} %copy.71, f32[2304]{0:T(1024)S(1)} %rsqrt.21, f32[2304]{0:T(1024)S(1)} %div.17), kind=kLoop, calls=%fused_computation.10 | loop fusion | flops 884736 | bytes 1787904 | tf_op jit(solution)/shard_map/convert_element_type | solution.py:161
  161.8 1.1 fusion.1
  (38 shorter events, 2.3 us)
Async XLA Ops:
  6.5 155.2 %copy-start = (bf16[128,128]{1,0:T(8,128)(2,1)S(1)}, bf16[128,128]{1,0:T(8,128)(2,1)}, u32[]{:S(2)}) copy-start(bf16[128,128]{1,0:T(8,128)(2,1)} %param.13) | copy-start | bytes 98308
  6.5 3.8 %copy-start.6 = (bf16[256,32]{0,1:T(8,128)(2,1)S(1)}, bf16[256,32]{0,1:T(8,128)(2,1)}, u32[]{:S(2)}) copy-start(bf16[256,32]{0,1:T(8,128)(2,1)} %param.10) | copy-start | bytes 49156
  10.4 20.5 %copy-start.7 = (bf16[256,32]{0,1:T(8,128)(2,1)S(1)}, bf16[256,32]{0,1:T(8,128)(2,1)}, u32[]{:S(2)}) copy-start(bf16[256,32]{0,1:T(8,128)(2,1)} %param.9) | copy-start | bytes 49156
  26.5 5.1 %copy-start.4 = (bf16[1024,128]{1,0:T(8,128)(2,1)S(1)}, bf16[1024,128]{1,0:T(8,128)(2,1)}, u32[]{:S(2)}) copy-start(bf16[1024,128]{1,0:T(8,128)(2,1)} %param.11) | copy-start | bytes 786436
  26.7 5.9 %copy-start.5 = (bf16[128,640]{1,0:T(8,128)(2,1)S(1)}, bf16[128,640]{1,0:T(8,128)(2,1)}, u32[]{:S(2)}) copy-start(bf16[128,640]{1,0:T(8,128)(2,1)} %param.12) | copy-start | bytes 491524
  27.4 13.4 %all-to-all-start = ((bf16[4,16,3072]{2,1,0:T(8,128)(2,1)}), bf16[4,16,3072]{2,1,0:T(8,128)(2,1)S(1)}, u32[]{:S(2)}, u32[]{:S(2)}) async-start(bf16[4,16,3072]{2,1,0:T(8,128)(2,1)} %bitcast.2), calls=%async_computation | async-start | bytes 786432 | tf_op jit(solution)/shard_map/all_to_all | solution.py:130
  40.8 0.7 copy-start.2
  83.3 24.4 %all-to-all-start.2 = ((bf16[128,24,96]{2,1,0:T(8,128)(2,1)}), bf16[128,24,96]{2,1,0:T(8,128)(2,1)S(1)}, u32[]{:S(2)}, u32[]{:S(2)}) async-start(bf16[128,24,96]{2,1,0:T(8,128)(2,1)} %get-tuple-element.12), calls=%async_computation.2 | async-start | bytes 1572864 | tf_op jit(solution)/shard_map/all_to_all | solution.py:150
  86.9 39.7 %all-gather.2.cloned.1.call-start = ((), (), s32[]{:S(2)}) async-start(), calls=%async_computation.5 | async-start | bytes 2359296 | tf_op jit(solution)/shard_map/all_gather | solution.py:155
  128.8 6.0 %copy-start.3 = (bf16[24,128,96]{2,1,0:T(8,128)(2,1)S(1)}, bf16[24,128,96]{2,1,0:T(8,128)(2,1)}, u32[]{:S(2)}) copy-start(bf16[24,128,96]{2,1,0:T(8,128)(2,1)} %get-tuple-element.9) | copy-start | bytes 1769476
  130.2 25.7 %all-to-all-start.4 = ((bf16[16,192,96]{2,0,1:T(8,128)(2,1)}), bf16[16,192,96]{2,0,1:T(8,128)(2,1)}, u32[]{:S(2)}, u32[]{:S(2)}) async-start(bf16[16,192,96]{2,0,1:T(8,128)(2,1)} %copy.69), calls=%async_computation.4 | async-start | bytes 1572864 | tf_op jit(solution)/shard_map/all_to_all | solution.py:159
  159.3 2.5 %copy-start.1 = (f32[24,96,128]{2,1,0:T(8,128)S(1)}, f32[24,96,128]{2,1,0:T(8,128)}, u32[]{:S(2)}) copy-start(f32[24,96,128]{2,1,0:T(8,128)} %copy.61) | copy-start | bytes 3538948
Sparse Core Ops, SparseCore 0:
  89.2 31.2 all-gather.1
